TPU v7x, 128 devices: a whole 4x4x4 slice. The times are simulated.
128 devices in a mesh: expert: 16 (over x, y_hi, core), dp: 8 (over y_lo, z).
Axes of the slice: x: 4, y: 4 (y_hi: 2, y_lo: 2; y = y_hi * 2 + y_lo), z: 4, core: 2. Of those that a mesh axis runs over, the one named last changes fastest.
Arguments:
- attn_rows: bfloat16 [16384, 7168], P('dp', 'expert'), may hold values from -6 to 6
- out_grad: bfloat16 [16384, 7168], P('dp', 'expert'), may hold values from -6 to 6
- routes: int32 [16384, 8], P(('dp', 'expert')), may hold values from 0 to 255, as said below
- gates: bfloat16 [16384, 8], P(('dp', 'expert')), may hold values from 0.049804688 to 0.5
- w_gate: bfloat16 [16, 7168, 2048], P('expert', None, 'dp'), may hold values from -0.0625 to 0.0625
- w_up: bfloat16 [16, 7168, 2048], P('expert', None, 'dp'), may hold values from -0.0625 to 0.0625
- w_down: bfloat16 [16, 2048, 7168], P('expert', 'dp'), may hold values from -0.125 to 0.125
Outputs:
- grad_input: bfloat16 [16384, 7168], P('dp', 'expert')
- grad_w_gate: bfloat16 [16, 7168, 2048], P('expert', None, 'dp')
- grad_w_up: bfloat16 [16, 7168, 2048], P('expert', None, 'dp')
Inputs may be any that keep to these rules, and one draw needn't show every extreme that they name: `routes`: each row names 8 different experts. In the 128 rows of one device (aligned blocks of 128 rows) no window expert (below 16) is named by more than 6 rows; in every device's rows some window expert is named by exactly 6 rows, and one window expert is named by exactly 6 rows of every device.
All inputs are finite; a program needn't handle non-finite values.
Results may differ from a plain program's by a relative error of at most 0.0058.
Values may be sent and summed in bfloat16 or wider, within the bound.
A program may use at most 256 MiB of HBM per device.

v0:
```python
import jax
import jax.numpy as jnp
from jax import lax
from jax.sharding import PartitionSpec as P

BF = jnp.bfloat16
F32 = jnp.float32


def slot_tables(routes, gates, experts, capacity):
    matches = (routes[..., None] == jnp.arange(experts, dtype=routes.dtype)).astype(F32)
    per_token = jnp.sum(matches, axis=2)
    coef = jnp.sum(matches * gates[..., None].astype(F32), axis=2)
    tokens = routes.shape[1]
    earlier = (jnp.arange(tokens)[:, None] < jnp.arange(tokens)[None, :]).astype(BF)
    before = jnp.einsum("bse,st->bte", per_token.astype(BF), earlier, preferred_element_type=F32)
    slot = jnp.arange(capacity, dtype=F32)
    hit = (before[..., None] == slot) & (per_token[..., None] > 0)
    hit = jnp.transpose(hit, (0, 2, 3, 1))
    scaled = jnp.where(hit, jnp.transpose(coef, (0, 2, 1))[:, :, None, :], 0.0)
    return (hit.astype(BF), scaled.astype(BF))


def per_device(attn_rows, out_grad, routes, gates, w_gate, w_up, w_down):
    experts = lax.axis_size("expert")
    groups = lax.axis_size("dp")
    own = routes.shape[0]
    capacity = 3 * own // 64
    width = attn_rows.shape[1]
    packed = jnp.concatenate([routes.astype(BF), gates], axis=1)
    packed = lax.all_gather(packed, "expert", axis=0, tiled=False)
    top = routes.shape[1]
    place, scaled = slot_tables(packed[..., :top], packed[..., top:], experts, capacity)

    def dispatch(table, rows):
        rows = rows.reshape(experts, own, width)
        sent = jnp.einsum("bect,btd->ebcd", table, rows, preferred_element_type=F32).astype(BF)
        sent = sent.reshape(experts, experts * capacity, width)
        got = lax.all_to_all(sent, "expert", split_axis=0, concat_axis=0, tiled=True)
        got = jnp.transpose(got, (1, 0, 2)).reshape(experts * capacity, experts * width)
        return lax.all_gather(got, "dp", axis=0, tiled=True)

    x = dispatch(place, attn_rows)
    dy = dispatch(scaled, out_grad)
    gate_mat, up_mat, down_mat = (w_gate[0], w_up[0], w_down[0])
    rows_dims = (((1,), (1,)), ((), ()))
    first_dims = (((0,), (0,)), ((), ()))
    g = jnp.dot(x, gate_mat, preferred_element_type=F32)
    u = jnp.dot(x, up_mat, preferred_element_type=F32)
    gh = lax.dot_general(dy, down_mat, rows_dims, preferred_element_type=F32)
    s = jax.nn.sigmoid(g)
    dg = (gh * u * s * (1.0 + g * (1.0 - s))).astype(BF)
    du = (gh * (g * s)).astype(BF)
    part = lax.dot_general(dg, gate_mat, rows_dims, preferred_element_type=F32)
    part = (part + lax.dot_general(du, up_mat, rows_dims, preferred_element_type=F32)).astype(BF)
    back = lax.psum_scatter(part, "dp", scatter_dimension=0, tiled=True)
    g_gate = lax.dot_general(x, dg, first_dims, preferred_element_type=F32).astype(BF)
    g_up = lax.dot_general(x, du, first_dims, preferred_element_type=F32).astype(BF)
    back = back.reshape(experts * capacity, experts, width)
    back = jnp.transpose(back, (1, 0, 2))
    back = lax.all_to_all(back, "expert", split_axis=0, concat_axis=0, tiled=True)
    back = back.reshape(experts, experts, capacity, width)
    grad_input = jnp.einsum("bect,ebcd->btd", place, back, preferred_element_type=F32).astype(BF)
    return (grad_input.reshape(experts * own, width), g_gate[None], g_up[None])


def solution(mesh):
    return jax.shard_map(
        per_device,
        mesh=mesh,
        in_specs=(
            P("dp", "expert"),
            P("dp", "expert"),
            P(("dp", "expert"), None),
            P(("dp", "expert"), None),
            P("expert", None, "dp"),
            P("expert", None, "dp"),
            P("expert", "dp", None),
        ),
        out_specs=(P("dp", "expert"), P("expert", None, "dp"), P("expert", None, "dp")),
        check_vma=False,
    )
```

profile of v0, /device:TPU:1, one launch (start us, length us, event | category | flops | bytes accessed | tf_op | source)
XLA Modules:
  0.0 514.2 jit_solution(15024579949341409885)
XLA Ops:
  7.2 0.7 convert_element_type.48
  8.6 25.8 %all-gather = bf16[2048,16]{0,1:T(8,128)(2,1)S(1)} all-gather(bf16[128,16]{0,1:T(8,128)(2,1)S(1)} %pad_maximum_fusion), channel_id=2, replica_groups=mesh['expert'=16,'dp'=8] {'expert'}, dimensions={0}, use_global_device_ids=true | all-gather | bytes 69632 | tf_op jit(solution)/shard_map/all_gather | solution.py:31
  34.4 0.8 convert_reduce_fusion
  35.5 2.0 copy.62
  37.5 0.9 fusion.18
  38.4 0.9 copy.45
  39.3 25.1 %all_to_all.15 = bf16[16,96,448]{2,1,0:T(8,128)(2,1)S(1)} all-to-all(bf16[16,96,448]{2,1,0:T(8,128)(2,1)S(1)} %copy.45), channel_id=1, replica_groups=mesh['expert'=16,'dp'=8] {'expert'}, dimensions={0} | all-to-all | bytes 2752512 | tf_op jit(solution)/shard_map/all_to_all | solution.py:39
  64.4 0.9 copy.46
  65.3 2.7 reshape.47
  68.8 0.9 fusion.15
  69.7 0.9 copy.42
  70.6 29.3 %all_to_all.16 = bf16[16,96,448]{2,1,0:T(8,128)(2,1)S(1)} all-to-all(bf16[16,96,448]{2,1,0:T(8,128)(2,1)S(1)} %copy.42), channel_id=1, replica_groups=mesh['expert'=16,'dp'=8] {'expert'}, dimensions={0} | all-to-all | bytes 2752512 | tf_op jit(solution)/shard_map/all_to_all | solution.py:39
  99.9 0.9 copy.43
  100.8 2.7 reshape.44
  103.7 96.4 %all-gather.6.cloned.1.call-done = bf16[768,7168]{1,0:T(8,128)(2,1)} async-done(((bf16[96,7168]{1,0:T(8,128)(2,1)}), bf16[768,7168]{1,0:T(8,128)(2,1)}) %all-gather.6.cloned.1.call-update) | async-done | bytes 11010064 | tf_op jit(solution)/shard_map/all_gather | solution.py:41
  200.1 6.9 %fusion.4 = f32[768,256]{1,0:T(8,128)S(1)} fusion(bf16[768,7168]{1,0:T(8,128)(2,1)} %all-gather.6.cloned.1.call-done, bf16[1,7168,256]{2,1,0:T(8,128)(2,1)} %param.11), kind=kOutput, calls=%fused_computation.8 | convolution fusion | flops 2818572288 | bytes 15466496 | tf_op jit(solution)/shard_map/dot_general | solution.py:48
  207.0 110.1 %all-gather.4.cloned.1.call-done = bf16[768,7168]{1,0:T(8,128)(2,1)} async-done(((bf16[96,7168]{1,0:T(8,128)(2,1)}), bf16[768,7168]{1,0:T(8,128)(2,1)}) %all-gather.4.cloned.1.call-update) | async-done | bytes 11010064 | tf_op jit(solution)/shard_map/all_gather | solution.py:41
  317.2 7.1 %multiply_convert_fusion = (bf16[768,256]{1,0:T(8,128)(2,1)S(1)}, f32[768,256]{1,0:T(8,128)S(1)}) fusion(f32[768,256]{1,0:T(8,128)S(1)} %fusion.4, bf16[768,7168]{1,0:T(8,128)(2,1)} %all-gather.4.cloned.1.call-done, bf16[1,256,7168]{2,1,0:T(8,128)(2,1)} %param.13), kind=kOutput, calls=%fused_computation.30 | convolution fusion | flops 2819751936 | bytes 16646144 | tf_op jit(solution)/shard_map/dot_general | solution.py:50
  324.3 2.4 copy-done.6
  326.6 4.5 fusion.31
  331.1 9.1 %fusion.2 = f32[768,7168]{1,0:T(8,128)} fusion(bf16[768,256]{1,0:T(8,128)(2,1)S(1)} %fusion.31, bf16[1,7168,256]{2,1,0:T(8,128)(2,1)S(1)} %copy-done.1), kind=kOutput, calls=%fused_computation.6 | convolution fusion | flops 2818572288 | bytes 26083328 | tf_op jit(solution)/shard_map/dot_general | solution.py:54
  340.2 12.6 %add_convert_fusion = bf16[768,7168]{1,0:T(8,128)(2,1)} fusion(f32[768,7168]{1,0:T(8,128)} %fusion.2, bf16[768,256]{1,0:T(8,128)(2,1)S(1)} %get-tuple-element.7, bf16[1,7168,256]{2,1,0:T(8,128)(2,1)S(1)} %copy-done), kind=kOutput, calls=%fused_computation | convolution fusion | flops 2829582336 | bytes 37093376 | tf_op jit(solution)/shard_map/dot_general | solution.py:55
  352.8 116.6 %reduce-scatter.2.cloned.1.call-done = bf16[96,7168]{1,0:T(8,128)(2,1)} async-done(((bf16[768,7168]{1,0:T(8,128)(2,1)}), bf16[96,7168]{1,0:T(8,128)(2,1)}) %reduce-scatter.2.cloned.1.call-update) | async-done | bytes 1376272 | tf_op jit(solution)/shard_map/reduce_scatter | solution.py:56
  469.3 3.1 reshape.48
  472.5 2.0 copy.75
  474.5 7.1 %all-to-all-start.2 = ((bf16[16,96,448]{2,1,0:T(8,128)(2,1)}), bf16[16,96,448]{2,1,0:T(8,128)(2,1)S(1)}, u32[]{:S(2)}, u32[]{:S(2)}) async-start(bf16[16,96,448]{2,1,0:T(8,128)(2,1)} %bitcast.80), calls=%async_computation.3 | async-start | bytes 3145728 | tf_op jit(solution)/shard_map/all_to_all | solution.py:61
  481.6 9.1 %fusion = bf16[1,7168,256]{2,1,0:T(8,128)(2,1)} fusion(bf16[768,7168]{1,0:T(8,128)(2,1)} %all-gather.6.cloned.1.call-done, bf16[768,256]{1,0:T(8,128)(2,1)S(1)} %fusion.31), kind=kOutput, calls=%fused_computation.3 | convolution fusion | flops 2820407296 | bytes 15073280 | tf_op jit(solution)/shard_map/dot_general | solution.py:57
  490.7 9.1 %fusion.1 = bf16[1,7168,256]{2,1,0:T(8,128)(2,1)} fusion(bf16[768,7168]{1,0:T(8,128)(2,1)} %all-gather.6.cloned.1.call-done, bf16[768,256]{1,0:T(8,128)(2,1)S(1)} %get-tuple-element.7), kind=kOutput, calls=%fused_computation.4 | convolution fusion | flops 2820407296 | bytes 15073280 | tf_op jit(solution)/shard_map/dot_general | solution.py:58
  499.8 4.6 all-to-all-done.2
  504.3 0.9 copy.48
  505.2 0.8 fusion.21
  506.0 1.7 copy.74
  (29 shorter events, 2.0 us)
Async XLA Ops:
  7.2 193.0 %all-gather.6.cloned.1.call-start = ((), (), s32[]{:S(2)}) async-start(), calls=%async_computation.5 | async-start | bytes 12386304 | tf_op jit(solution)/shard_map/all_gather | solution.py:41
  35.3 3.1 copy-start.3
  64.4 3.6 copy-start.2
  68.0 0.8 copy-start.4
  68.0 0.9 copy-start.5
  68.0 249.2 %all-gather.4.cloned.1.call-start = ((), (), s32[]{:S(2)}) async-start(), calls=%async_computation.4 | async-start | bytes 12386304 | tf_op jit(solution)/shard_map/all_gather | solution.py:41
  103.5 365.8 %reduce-scatter.2.cloned.1.call-start = ((), (), s32[]{:S(2)}) async-start(), calls=%async_computation.6 | async-start | bytes 12386304 | tf_op jit(solution)/shard_map/reduce_scatter | solution.py:56
  207.0 117.3 %copy-start.7 = (f32[768,256]{1,0:T(8,128)}, f32[768,256]{1,0:T(8,128)S(1)}, u32[]{:S(2)}) copy-start(f32[768,256]{1,0:T(8,128)S(1)} %fusion.4) | copy-start | bytes 2359300
  317.2 7.1 %copy-start = (bf16[1,7168,256]{2,1,0:T(8,128)(2,1)S(1)}, bf16[1,7168,256]{2,1,0:T(8,128)(2,1)}, u32[]{:S(2)}) copy-start(bf16[1,7168,256]{2,1,0:T(8,128)(2,1)} %param.12) | copy-start | bytes 11010052
  317.2 9.5 %copy-start.6 = (bf16[768,7168]{1,0:T(8,128)(2,1)S(1)}, bf16[768,7168]{1,0:T(8,128)(2,1)}, u32[]{:S(2)}) copy-start(bf16[768,7168]{1,0:T(8,128)(2,1)} %all-gather.6.cloned.1.call-done) | copy-start | bytes 33030148
  326.6 4.5 copy-start.1
  474.5 29.8 %all-to-all-start.2 = ((bf16[16,96,448]{2,1,0:T(8,128)(2,1)}), bf16[16,96,448]{2,1,0:T(8,128)(2,1)S(1)}, u32[]{:S(2)}, u32[]{:S(2)}) async-start(bf16[16,96,448]{2,1,0:T(8,128)(2,1)} %bitcast.80), calls=%async_computation.3 | async-start | bytes 3145728 | tf_op jit(solution)/shard_map/all_to_all | solution.py:61
Sparse Core Ops, SparseCore 0:
  68.1 131.9 all-gather.5
  202.3 114.7 all-gather.3
  352.9 116.4 reduce-scatter.1
where the time goes:
time: 515 us; the launch traced here: 514 us
  waiting for transfers between devices  328 us (64%)
  blocking collectives  80.2 us (16%)
  matrix products  60.9 us (12%)
  local copies, waits for them, and re-layouts  21.8 us (4%)
  between operations  13.9 us (3%)
  starting transfers between devices  7.45 us (1%)
    all_gather x2, waiting for transfers between devices, dispatch(): return lax.all_gather(got, 'dp', axis=0, tiled=True)  207 us
    reduce_scatter x1, waiting for transfers between devices, per_device(): back = lax.psum_scatter(part, 'dp', scatter_dimension=0, tiled=True)  117 us
    all_to_all x2, blocking collectives, dispatch(): lax.all_to_all(sent, 'expert', split_axis=0, concat_axis=0, tiled=True)  54.4 us
    all_gather x1, blocking collectives, per_device(): packed = lax.all_gather(packed, 'expert', axis=0, tiled=False)  25.8 us
    dot_general x1, matrix products, per_device(): lax.dot_general(du, up_mat, rows_dims, preferred_element_type=F32)  12.6 us
  transfers between devices with their start and end apart: 4, of which 4 were waited for; matrix products, arithmetic and copies ran while one was open for 6% of the time, Pallas kernels for 0%

commit v1 on v0

--- a/solution.py
+++ b/solution.py
@@ -38,7 +38,9 @@
         sent = sent.reshape(experts, experts * capacity, width)
         got = lax.all_to_all(sent, "expert", split_axis=0, concat_axis=0, tiled=True)
         got = jnp.transpose(got, (1, 0, 2)).reshape(experts * capacity, experts * width)
-        return lax.all_gather(got, "dp", axis=0, tiled=True)
+        return jnp.concatenate(
+            lax.all_to_all(jnp.stack([got] * lax.axis_size("dp")), "dp", 0, 0), axis=0
+        )
 
     x = dispatch(place, attn_rows)
     dy = dispatch(scaled, out_grad)

time: 515 us -> 559 us (1.085)
  waiting for transfers between devices: 328 us -> 389 us
  blocking collectives: 80.2 us -> 25.8 us
  starting transfers between devices: 7.45 us -> 26.2 us
  local copies, waits for them, and re-layouts: 21.8 us -> 34.5 us
  matrix products: 60.9 us -> 66.9 us
    all_to_all x0 -> x4, waiting for transfers between devices: none -> 268 us  [the longest x2 233 us: dispatch(): lax.all_to_all(jnp.stack([got] * lax.axis_size('dp')), 'dp', 0, 0)]
    all_gather x2 -> x0, waiting for transfers between devices: 207 us -> none  [dispatch(): return lax.all_gather(got, 'dp', axis=0, tiled=True)]
    all_to_all x2 -> x0, blocking collectives: 54.4 us -> none  [dispatch(): lax.all_to_all(sent, 'expert', split_axis=0, concat_axis=0, tiled=True)]
    all_to_all x0 -> x4, starting transfers between devices: none -> 18.8 us  [the longest x2 10.4 us: dispatch(): lax.all_to_all(jnp.stack([got] * lax.axis_size('dp')), 'dp', 0, 0)]
    another operation x0 -> x4, local copies, waits for them, and re-layouts: none -> 15.8 us  [dispatch(): jnp.stack([got] * lax.axis_size('dp'))]
  transfers between devices with their start and end apart: 4 -> 6, of which waited for: 4 -> 6; matrix products, arithmetic and copies ran while one was open for 6% -> 7% of each run, Pallas kernels for 0% -> 0%
where the time goes in v1:
time: 559 us; the launch traced here: 558 us
  waiting for transfers between devices  389 us (70%)
  matrix products  66.9 us (12%)
  local copies, waits for them, and re-layouts  34.5 us (6%)
  starting transfers between devices  26.2 us (5%)
  blocking collectives  25.8 us (5%)
  between operations  14.2 us (3%)
    all_to_all x2, waiting for transfers between devices, dispatch(): lax.all_to_all(jnp.stack([got] * lax.axis_size('dp')), 'dp', 0, 0)  233 us
    reduce_scatter x1, waiting for transfers between devices, per_device(): back = lax.psum_scatter(part, 'dp', scatter_dimension=0, tiled=True)  116 us
    all_to_all x2, waiting for transfers between devices, dispatch(): lax.all_to_all(sent, 'expert', split_axis=0, concat_axis=0, tiled=True)  35.5 us
    all_gather x1, blocking collectives, per_device(): packed = lax.all_gather(packed, 'expert', axis=0, tiled=False)  25.8 us
    another operation x4, local copies, waits for them, and re-layouts, dispatch(): jnp.stack([got] * lax.axis_size('dp'))  15.8 us
    dot_general x1, matrix products, per_device(): lax.dot_general(du, up_mat, rows_dims, preferred_element_type=F32)  11.8 us
  transfers between devices with their start and end apart: 6, of which 6 were waited for; matrix products, arithmetic and copies ran while one was open for 7% of the time, Pallas kernels for 0%

profile of v1, /device:TPU:1, one launch (start us, length us, event | category | flops | bytes accessed | tf_op | source)
XLA Modules:
  0.0 557.9 jit_solution(6037718442242459409)
XLA Ops:
  8.5 25.8 %all-gather = bf16[2048,16]{0,1:T(8,128)(2,1)S(1)} all-gather(bf16[128,16]{0,1:T(8,128)(2,1)S(1)} %pad_maximum_fusion), channel_id=2, replica_groups=mesh['expert'=16,'dp'=8] {'expert'}, dimensions={0}, use_global_device_ids=true | all-gather | bytes 69632 | tf_op jit(solution)/shard_map/all_gather | solution.py:31
  34.8 2.0 copy.62
  37.7 2.0 copy.45
  39.8 3.7 all-to-all-start.2
  43.4 2.0 copy.61
  45.4 0.9 fusion.15
  46.4 2.0 copy.42
  48.4 17.8 %all-to-all-done.2 = bf16[16,96,448]{2,1,0:T(8,128)(2,1)S(1)} async-done(((bf16[16,96,448]{2,1,0:T(8,128)(2,1)}), bf16[16,96,448]{2,1,0:T(8,128)(2,1)S(1)}, u32[]{:S(2)}, u32[]{:S(2)}) %all-to-all-start.2) | async-done | bytes 1376288 | tf_op jit(solution)/shard_map/all_to_all | solution.py:39
  66.2 4.8 all-to-all-start
  71.0 2.0 copy.46
  73.0 3.0 stack_reshape.5
  76.0 17.7 %all-to-all-done = bf16[16,96,448]{2,1,0:T(8,128)(2,1)S(1)} async-done(((bf16[16,96,448]{2,1,0:T(8,128)(2,1)}), bf16[16,96,448]{2,1,0:T(8,128)(2,1)S(1)}, u32[]{:S(2)}, u32[]{:S(2)}) %all-to-all-start) | async-done | bytes 1376288 | tf_op jit(solution)/shard_map/all_to_all | solution.py:39
  93.7 5.5 stack.7
  99.2 5.2 all-to-all-start.3
  105.3 1.8 stack_reshape.4
  107.2 120.3 %all-to-all-done.3 = bf16[8,96,7168]{2,1,0:T(8,128)(2,1)} async-done(((bf16[8,96,7168]{2,1,0:T(8,128)(2,1)}), bf16[8,96,7168]{2,1,0:T(8,128)(2,1)}, u32[]{:S(2)}, u32[]{:S(2)}) %all-to-all-start.3) | async-done | bytes 11010080 | tf_op jit(solution)/shard_map/all_to_all | solution.py:42
  227.4 5.4 stack.6
  232.8 5.2 all-to-all-start.1
  238.2 9.1 %fusion.4 = f32[768,256]{1,0:T(8,128)} fusion(bf16[768,7168]{1,0:T(8,128)(2,1)} %bitcast.13, bf16[1,7168,256]{2,1,0:T(8,128)(2,1)} %param.11), kind=kOutput, calls=%fused_computation.8 | convolution fusion | flops 2818572288 | bytes 15466496 | tf_op jit(solution)/shard_map/dot_general | solution.py:50
  247.3 112.4 %all-to-all-done.1 = bf16[8,96,7168]{2,1,0:T(8,128)(2,1)} async-done(((bf16[8,96,7168]{2,1,0:T(8,128)(2,1)}), bf16[8,96,7168]{2,1,0:T(8,128)(2,1)}, u32[]{:S(2)}, u32[]{:S(2)}) %all-to-all-start.1) | async-done | bytes 11010080 | tf_op jit(solution)/shard_map/all_to_all | solution.py:42
  359.7 8.6 %multiply_convert_fusion = (bf16[768,256]{1,0:T(8,128)(2,1)S(1)}, f32[768,256]{1,0:T(8,128)S(1)}) fusion(f32[768,256]{1,0:T(8,128)} %fusion.4, bf16[768,7168]{1,0:T(8,128)(2,1)} %bitcast.7, bf16[1,256,7168]{2,1,0:T(8,128)(2,1)} %param.13), kind=kOutput, calls=%fused_computation.30 | convolution fusion | flops 2819751936 | bytes 16646144 | tf_op jit(solution)/shard_map/dot_general | solution.py:52
  368.3 7.4 %fusion.31 = bf16[768,256]{1,0:T(8,128)(2,1)S(1)} fusion(f32[768,256]{1,0:T(8,128)S(1)} %get-tuple-element.8, bf16[768,7168]{1,0:T(8,128)(2,1)} %bitcast.13, bf16[1,7168,256]{2,1,0:T(8,128)(2,1)S(1)} %copy-done, f32[768,256]{1,0:T(8,128)S(1)} %copy-done.2), kind=kOutput, calls=%fused_computation.27 | convolution fusion | flops 2820538368 | bytes 16646144 | tf_op jit(solution)/shard_map/dot_general | solution.py:51
  375.7 9.2 %fusion.2 = f32[768,7168]{1,0:T(8,128)} fusion(bf16[768,256]{1,0:T(8,128)(2,1)S(1)} %fusion.31, bf16[1,7168,256]{2,1,0:T(8,128)(2,1)S(1)} %copy-done.1), kind=kOutput, calls=%fused_computation.6 | convolution fusion | flops 2818572288 | bytes 26083328 | tf_op jit(solution)/shard_map/dot_general | solution.py:56
  384.9 11.8 %add_convert_fusion = bf16[768,7168]{1,0:T(8,128)(2,1)} fusion(f32[768,7168]{1,0:T(8,128)} %fusion.2, bf16[768,256]{1,0:T(8,128)(2,1)S(1)} %get-tuple-element.7, bf16[1,7168,256]{2,1,0:T(8,128)(2,1)S(1)} %copy-done), kind=kOutput, calls=%fused_computation | convolution fusion | flops 2829582336 | bytes 37093376 | tf_op jit(solution)/shard_map/dot_general | solution.py:57
  396.7 115.9 %reduce-scatter.2.cloned.1.call-done = bf16[96,7168]{1,0:T(8,128)(2,1)} async-done(((bf16[768,7168]{1,0:T(8,128)(2,1)}), bf16[96,7168]{1,0:T(8,128)(2,1)}) %reduce-scatter.2.cloned.1.call-update) | async-done | bytes 1376272 | tf_op jit(solution)/shard_map/reduce_scatter | solution.py:58
  512.7 3.1 reshape.52
  515.8 2.0 copy.75
  517.8 7.2 %all-to-all-start.4 = ((bf16[16,96,448]{2,1,0:T(8,128)(2,1)}), bf16[16,96,448]{2,1,0:T(8,128)(2,1)S(1)}, u32[]{:S(2)}, u32[]{:S(2)}) async-start(bf16[16,96,448]{2,1,0:T(8,128)(2,1)} %bitcast.82), calls=%async_computation.5 | async-start | bytes 3145728 | tf_op jit(solution)/shard_map/all_to_all | solution.py:63
  525.0 9.1 %fusion = bf16[1,7168,256]{2,1,0:T(8,128)(2,1)} fusion(bf16[768,7168]{1,0:T(8,128)(2,1)} %bitcast.13, bf16[768,256]{1,0:T(8,128)(2,1)S(1)} %fusion.31), kind=kOutput, calls=%fused_computation.3 | convolution fusion | flops 2820407296 | bytes 15073280 | tf_op jit(solution)/shard_map/dot_general | solution.py:59
  534.1 9.1 %fusion.1 = bf16[1,7168,256]{2,1,0:T(8,128)(2,1)} fusion(bf16[768,7168]{1,0:T(8,128)(2,1)} %bitcast.13, bf16[768,256]{1,0:T(8,128)(2,1)S(1)} %get-tuple-element.7), kind=kOutput, calls=%fused_computation.4 | convolution fusion | flops 2820407296 | bytes 15073280 | tf_op jit(solution)/shard_map/dot_general | solution.py:60
  543.1 4.5 all-to-all-done.4
  549.3 1.7 copy.74
  (21 shorter events, 5.5 us)
Async XLA Ops:
  39.8 26.4 %all-to-all-start.2 = ((bf16[16,96,448]{2,1,0:T(8,128)(2,1)}), bf16[16,96,448]{2,1,0:T(8,128)(2,1)S(1)}, u32[]{:S(2)}, u32[]{:S(2)}) async-start(bf16[16,96,448]{2,1,0:T(8,128)(2,1)} %copy.45), calls=%async_computation.2 | async-start | bytes 3145728 | tf_op jit(solution)/shard_map/all_to_all | solution.py:39
  66.2 27.5 %all-to-all-start = ((bf16[16,96,448]{2,1,0:T(8,128)(2,1)}), bf16[16,96,448]{2,1,0:T(8,128)(2,1)S(1)}, u32[]{:S(2)}, u32[]{:S(2)}) async-start(bf16[16,96,448]{2,1,0:T(8,128)(2,1)} %copy.42), calls=%async_computation | async-start | bytes 3145728 | tf_op jit(solution)/shard_map/all_to_all | solution.py:39
  99.2 128.2 %all-to-all-start.3 = ((bf16[8,96,7168]{2,1,0:T(8,128)(2,1)}), bf16[8,96,7168]{2,1,0:T(8,128)(2,1)}, u32[]{:S(2)}, u32[]{:S(2)}) async-start(bf16[8,96,7168]{2,1,0:T(8,128)(2,1)} %stack.7), calls=%async_computation.3 | async-start | bytes 22020096 | tf_op jit(solution)/shard_map/all_to_all | solution.py:42
  232.8 126.9 %all-to-all-start.1 = ((bf16[8,96,7168]{2,1,0:T(8,128)(2,1)}), bf16[8,96,7168]{2,1,0:T(8,128)(2,1)}, u32[]{:S(2)}, u32[]{:S(2)}) async-start(bf16[8,96,7168]{2,1,0:T(8,128)(2,1)} %stack.6), calls=%async_computation.1 | async-start | bytes 22020096 | tf_op jit(solution)/shard_map/all_to_all | solution.py:42
  238.0 274.7 %reduce-scatter.2.cloned.1.call-start = ((), (), s32[]{:S(2)}) async-start(), calls=%async_computation.6 | async-start | bytes 12386304 | tf_op jit(solution)/shard_map/reduce_scatter | solution.py:58
  359.7 8.6 %copy-start = (bf16[1,7168,256]{2,1,0:T(8,128)(2,1)S(1)}, bf16[1,7168,256]{2,1,0:T(8,128)(2,1)}, u32[]{:S(2)}) copy-start(bf16[1,7168,256]{2,1,0:T(8,128)(2,1)} %param.12) | copy-start | bytes 11010052
  359.7 8.6 %copy-start.2 = (f32[768,256]{1,0:T(8,128)S(1)}, f32[768,256]{1,0:T(8,128)}, u32[]{:S(2)}) copy-start(f32[768,256]{1,0:T(8,128)} %fusion.4) | copy-start | bytes 2359300
  368.3 7.5 %copy-start.1 = (bf16[1,7168,256]{2,1,0:T(8,128)(2,1)S(1)}, bf16[1,7168,256]{2,1,0:T(8,128)(2,1)}, u32[]{:S(2)}) copy-start(bf16[1,7168,256]{2,1,0:T(8,128)(2,1)} %param.11) | copy-start | bytes 11010052
  517.8 29.9 %all-to-all-start.4 = ((bf16[16,96,448]{2,1,0:T(8,128)(2,1)}), bf16[16,96,448]{2,1,0:T(8,128)(2,1)S(1)}, u32[]{:S(2)}, u32[]{:S(2)}) async-start(bf16[16,96,448]{2,1,0:T(8,128)(2,1)} %bitcast.82), calls=%async_computation.5 | async-start | bytes 3145728 | tf_op jit(solution)/shard_map/all_to_all | solution.py:63
Sparse Core Ops, SparseCore 0:
  396.9 115.7 reduce-scatter.1
